TPU v7x, 256 devices: a whole 4x4x8 slice. The times are simulated.
256 devices in a mesh: space: 16 (over x_hi, z), tm: 16 (over x_lo, y, core).
Axes of the slice: x: 4 (x_hi: 2, x_lo: 2; x = x_hi * 2 + x_lo), y: 4, z: 8, core: 2. Of those that a mesh axis runs over, the one named last changes fastest.
Arguments:
- right_side: bfloat16 [16, 16, 4, 4, 64, 64], P('tm', 'space'), may hold values from -6 to 6
- batch_order: int32 [32], replicated, may hold values from 0 to 31, each once
- light_diag: bfloat16 [16, 16, 4, 4, 64, 128], P('tm', 'space'), may hold values from -1 to 2
- light_hops: bfloat16 [8, 16, 16, 4, 4, 64, 128], P(None, 'tm', 'space'), may hold values from -0.125 to 0.125
- charm_diag: bfloat16 [16, 16, 4, 4, 64, 128], P('tm', 'space'), may hold values from -1 to 2
- charm_hops: bfloat16 [8, 16, 16, 4, 4, 64, 128], P(None, 'tm', 'space'), may hold values from -0.125 to 0.125
- current_blocks: bfloat16 [16, 16, 4, 4, 64, 128], P('tm', 'space'), may hold values from -0.5 to 0.5
Outputs:
- light_field: bfloat16 [16, 16, 4, 4, 64, 64], P('tm', 'space')
- seq_field: bfloat16 [16, 16, 4, 4, 64, 64], P('tm', 'space')
- margin: float32 [2, 32, 32], replicated
All inputs are finite; a program needn't handle non-finite values.
Results may differ from a plain program's by a relative error of at most 0.015.
Values may be sent and summed in bfloat16 or wider, within the bound.
A program may use at most 64 MiB of HBM per device.

v0:
```python
import math

import jax
import jax.numpy as jnp
from jax import lax
from jax.experimental import pallas as pl
from jax.experimental.pallas import tpu as pltpu
from jax.sharding import PartitionSpec as P

BF = jnp.bfloat16
F32 = jnp.float32
MESH = pl.DeviceIdType.MESH

LX = 4
LY = 4
SITES = LX * LY
PAIRS = SITES // 2
NC = 64
COLS = 32
LANES = 4 * COLS
CHUNKS = 4
PER = PAIRS // CHUNKS
ROUNDS = 6

X_LO = 2
Y = 4
Z = 8
CORES = 2
X = 4
STAGES = ((CORES, 0), (Y, 2), (X, 6), (Z, 10))
SLOTS = 18


def sites_of(pair):
    x, h = divmod(pair, 2)
    return x * LY + h, x * LY + h + 2


def body_kernel(
    right_hbm, order_ref, ldiag_hbm, lhops_hbm, cdiag_hbm, chops_hbm, current_hbm,
    light_out, seq_out, margin_ref,
    right, ldiag, lhops, cdiag, chops, current,
    sent, halo, local, base, acc, light_t, light_v, seq_v, red,
    in_sem, out_sem, send_sem, recv_sem, red_send, red_recv,
):
    space = lax.axis_index("space")
    tm = lax.axis_index("tm")
    n_space = lax.axis_size("space")
    n_tm = lax.axis_size("tm")
    z = lax.rem(space, Z)
    core = lax.rem(tm, CORES)
    y = lax.rem(tm // CORES, Y)
    x = (space // Z) * X_LO + tm // (CORES * Y)

    def device(x_, y_, z_, core_):
        return ((x_ // X_LO) * Z + z_, (lax.rem(x_, X_LO) * Y + y_) * CORES + core_)

    def partner(stage, step):
        if stage == 0:
            return device(x, y, z, lax.rem(core + step, CORES))
        if stage == 1:
            return device(x, lax.rem(y + step, Y), z, core)
        if stage == 2:
            return device(lax.rem(x + step, X), y, z, core)
        return device(x, y, lax.rem(z + step, Z), core)

    takers = (
        (lax.rem(space + n_space - 1, n_space), tm),
        (lax.rem(space + 1, n_space), tm),
        (space, lax.rem(tm + n_tm - 1, n_tm)),
        (space, lax.rem(tm + 1, n_tm)),
    )

    loads = [
        pltpu.make_async_copy(src, dst, in_sem.at[i])
        for i, (src, dst) in enumerate((
            (right_hbm, right),
            (ldiag_hbm, ldiag),
            (lhops_hbm.at[pl.ds(0, 4)], lhops.at[pl.ds(0, 4)]),
            (lhops_hbm.at[pl.ds(4, 4)], lhops.at[pl.ds(4, 4)]),
            (current_hbm, current),
            (cdiag_hbm, cdiag),
            (chops_hbm.at[pl.ds(0, 4)], chops.at[pl.ds(0, 4)]),
            (chops_hbm.at[pl.ds(4, 4)], chops.at[pl.ds(4, 4)]),
        ))
    ]
    for copy in loads:
        copy.start()

    barrier = pltpu.get_barrier_semaphore()
    greeted = list(takers)
    for stage, (count, _) in enumerate(STAGES):
        greeted += [partner(stage, step) for step in range(1, count)]
    for other in greeted:
        pl.semaphore_signal(barrier, inc=1, device_id=other, device_id_type=MESH)

    lane = lax.broadcasted_iota(jnp.int32, (NC, LANES), 1)
    first = lax.rem(lane, 2 * COLS) < COLS
    low = lane < 2 * COLS

    def turn(v):
        rolled = pltpu.roll(v, 2 * COLS, axis=1)
        return jnp.where(low, -rolled, rolled)

    def swap(v):
        return jnp.where(first, pltpu.roll(v, 3 * COLS, axis=1), pltpu.roll(v, COLS, axis=1))

    def product(blocks, widened):
        out = jnp.dot(blocks, widened, preferred_element_type=F32)
        return jnp.where(first, out[:NC], out[NC:])

    def pair_blocks(ref, pair):
        one, two = sites_of(pair)
        return jnp.concatenate([ref[one], ref[two]], axis=0)

    def hop_blocks(ref, pair, numbers):
        return jnp.concatenate([pair_blocks(ref.at[e], pair) for e in numbers], axis=1)

    def on_site(ref, pair, field32):
        v32 = field32.astype(BF).astype(F32)
        widened = jnp.concatenate([v32.astype(BF), turn(v32).astype(BF)], axis=0)
        return product(pair_blocks(ref, pair), widened)

    def keep(round_, pair, field32):
        v32 = field32.astype(BF).astype(F32)
        v = v32.astype(BF)
        sent[round_, pair] = v
        swapped = swap(v32)
        local[pair, 0] = jnp.concatenate([v, turn(v32).astype(BF)], axis=0)
        local[pair, 1] = jnp.concatenate(
            [swapped.astype(BF), turn(swapped).astype(BF)], axis=0
        )

    def halo_copy(round_, direction, chunk):
        part = pl.ds(chunk * PER, PER)
        return pltpu.make_async_remote_copy(
            src_ref=sent.at[round_, part],
            dst_ref=halo.at[round_, direction, part],
            send_sem=send_sem.at[round_, direction, chunk],
            recv_sem=recv_sem.at[round_, direction, chunk],
            device_id=takers[direction],
            device_id_type=MESH,
        )

    def send(round_, chunk):
        for direction in range(4):
            halo_copy(round_, direction, chunk).start()

    def local_phase(hops):
        for pair in range(PAIRS):
            px, h = divmod(pair, 2)
            ahead = ((px + 1) % LX) * 2 + h
            behind = ((px - 1) % LX) * 2 + h
            beside = px * 2 + 1 - h
            widened = jnp.concatenate(
                [local[ahead, 0], local[behind, 0], local[beside, h], local[beside, 1 - h]], axis=0
            )
            acc[pair] = base[pair].astype(F32) + product(
                hop_blocks(hops, pair, (0, 1, 2, 3)), widened
            )

    def remote_pair(round_, hops, diag, pair):
        parts = []
        for direction in range(4):
            v = halo[round_, direction, pair]
            parts += [v, turn(v.astype(F32)).astype(BF)]
        residue = acc[pair] + product(
            hop_blocks(hops, pair, (4, 5, 6, 7)), jnp.concatenate(parts, axis=0)
        )
        return on_site(diag, pair, residue)

    def arrive(round_, chunk):
        for direction in range(4):
            halo_copy(round_, direction, chunk).wait_recv()

    def pairs_of(chunk):
        return range(chunk * PER, (chunk + 1) * PER)

    order = jnp.concatenate([order_ref[...]] * 4, axis=1)
    picked = order + jnp.where(low[:1], 0, COLS)
    row = lax.broadcasted_iota(jnp.int32, (2 * COLS, LANES), 0)
    hit = row == picked
    pick_one = jnp.where(jnp.logical_and(hit, first), 1.0, 0.0).astype(BF)
    pick_two = jnp.where(jnp.logical_and(hit, jnp.logical_not(first)), 1.0, 0.0).astype(BF)
    pick = jnp.concatenate([pick_one, pick_two], axis=0)

    loads[0].wait()
    loads[1].wait()
    for chunk in range(CHUNKS):
        for pair in pairs_of(chunk):
            one, two = sites_of(pair)
            both = jnp.dot(right[one], pick_one, preferred_element_type=F32) + jnp.dot(
                right[two], pick_two, preferred_element_type=F32
            )
            base[pair] = both.astype(BF)
            keep(0, pair, on_site(ldiag, pair, both))
        if chunk == 0:
            pl.semaphore_wait(barrier, SLOTS)
        send(0, chunk)
    loads[2].wait()
    loads[3].wait()

    def light_sweep(step, carry):
        local_phase(lhops)
        for chunk in range(CHUNKS):
            arrive(step, chunk)
            for pair in pairs_of(chunk):
                keep(step + 1, pair, remote_pair(step, lhops, ldiag, pair))
            send(step + 1, chunk)
        return carry

    lax.fori_loop(0, 2, light_sweep, 0)

    out_row = lax.broadcasted_iota(jnp.int32, (LANES, 2 * COLS), 0)
    out_col = lax.broadcasted_iota(jnp.int32, (LANES, 2 * COLS), 1)
    source_lane = lax.rem(out_col, COLS) + (out_col // COLS) * 2 * COLS
    take_one = jnp.where(out_row == source_lane, 1.0, 0.0).astype(BF)
    take_two = jnp.where(out_row == source_lane + COLS, 1.0, 0.0).astype(BF)

    def put(ref, pair, v):
        one, two = sites_of(pair)
        ref[one] = jnp.dot(v, take_one, preferred_element_type=F32).astype(BF)
        ref[two] = jnp.dot(v, take_two, preferred_element_type=F32).astype(BF)

    local_phase(lhops)
    for i in (4, 5):
        loads[i].wait()
    for chunk in range(CHUNKS):
        arrive(2, chunk)
        for pair in pairs_of(chunk):
            field = remote_pair(2, lhops, ldiag, pair)
            v = field.astype(BF)
            light_t[pair] = v
            inserted = on_site(current, pair, field)
            base[pair] = inserted.astype(BF)
            keep(3, pair, on_site(cdiag, pair, inserted))
        send(3, chunk)
    loads[6].wait()
    loads[7].wait()
    for pair in range(PAIRS):
        put(light_v, pair, light_t[pair])
    light_copy = pltpu.make_async_copy(light_v, light_out, out_sem.at[0])
    light_copy.start()

    def charm_sweep(step, carry):
        local_phase(chops)
        for chunk in range(CHUNKS):
            arrive(step, chunk)
            for pair in pairs_of(chunk):
                keep(step + 1, pair, remote_pair(step, chops, cdiag, pair))
            send(step + 1, chunk)
        return carry

    lax.fori_loop(3, 5, charm_sweep, 0)

    local_phase(chops)
    gram = jnp.zeros((LANES, LANES), F32)
    for chunk in range(CHUNKS):
        arrive(5, chunk)
        for pair in pairs_of(chunk):
            v = remote_pair(5, chops, cdiag, pair).astype(BF)
            gram = gram + lax.dot_general(
                light_t[pair], v, (((0,), (0,)), ((), ())), preferred_element_type=F32
            )
            put(seq_v, pair, v)
    seq_copy = pltpu.make_async_copy(seq_v, seq_out, out_sem.at[1])
    seq_copy.start()

    upper = gram[:COLS] + pltpu.roll(gram[COLS:2 * COLS], 3 * COLS, axis=1)
    lower = pltpu.roll(gram[2 * COLS:3 * COLS], 2 * COLS, axis=1) + pltpu.roll(
        gram[3 * COLS:], COLS, axis=1
    )
    sums = jnp.where(lane[:COLS] < COLS, upper + lower, upper - lower)
    half = COLS // 2
    total = jnp.where(
        first[:half], sums[:half], pltpu.roll(sums[half:], COLS, axis=1)
    )

    mine = (core, y, x, z)
    for stage, (count, offset) in enumerate(STAGES):
        me = mine[stage]
        red[offset + me] = total
        copies = []
        for step in range(1, count):
            copies.append(pltpu.make_async_remote_copy(
                src_ref=red.at[offset + me],
                dst_ref=red.at[offset + me],
                send_sem=red_send.at[offset + step],
                recv_sem=red_recv.at[offset + step],
                device_id=partner(stage, step),
                device_id_type=MESH,
            ))
        for copy in copies:
            copy.start()
        for copy in copies:
            copy.wait()
        total = red[offset]
        for slot in range(1, count):
            total = total + red[offset + slot]

    total = total * (1.0 / math.sqrt(n_space * n_tm * SITES * NC))
    margin_ref[0, :half] = total[:, :COLS]
    margin_ref[0, half:] = total[:, COLS:2 * COLS]
    margin_ref[1, :half] = total[:, 2 * COLS:3 * COLS]
    margin_ref[1, half:] = total[:, 3 * COLS:]

    light_copy.wait()
    seq_copy.wait()
    for round_ in range(ROUNDS):
        for chunk in range(CHUNKS):
            for direction in range(4):
                halo_copy(round_, direction, chunk).wait_send()


def body(right_side, batch_order, light_diag, light_hops, charm_diag, charm_hops, current_blocks):
    anywhere = pl.BlockSpec(memory_space=pl.ANY)
    vmem = pl.BlockSpec(memory_space=pltpu.VMEM)
    block = (SITES, NC, 2 * NC)
    field = (SITES, NC, 2 * COLS)
    hops = (8,) + block
    packed = (NC, LANES)
    light, seq, margin = pl.pallas_call(
        body_kernel,
        out_shape=(
            jax.ShapeDtypeStruct(field, BF),
            jax.ShapeDtypeStruct(field, BF),
            jax.ShapeDtypeStruct((2, COLS, COLS), F32),
        ),
        in_specs=[anywhere, vmem, anywhere, anywhere, anywhere, anywhere, anywhere],
        out_specs=(anywhere, anywhere, vmem),
        scratch_shapes=[
            pltpu.VMEM(field, BF),
            pltpu.VMEM(block, BF),
            pltpu.VMEM(hops, BF),
            pltpu.VMEM(block, BF),
            pltpu.VMEM(hops, BF),
            pltpu.VMEM(block, BF),
            pltpu.VMEM((ROUNDS, PAIRS) + packed, BF),
            pltpu.VMEM((ROUNDS, 4, PAIRS) + packed, BF),
            pltpu.VMEM((PAIRS, 2, 2 * NC, LANES), BF),
            pltpu.VMEM((PAIRS,) + packed, BF),
            pltpu.VMEM((PAIRS,) + packed, F32),
            pltpu.VMEM((PAIRS,) + packed, BF),
            pltpu.VMEM(field, BF),
            pltpu.VMEM(field, BF),
            pltpu.VMEM((SLOTS, COLS // 2, LANES), F32),
            pltpu.SemaphoreType.DMA((8,)),
            pltpu.SemaphoreType.DMA((2,)),
            pltpu.SemaphoreType.DMA((ROUNDS, 4, CHUNKS)),
            pltpu.SemaphoreType.DMA((ROUNDS, 4, CHUNKS)),
            pltpu.SemaphoreType.DMA((SLOTS,)),
            pltpu.SemaphoreType.DMA((SLOTS,)),
        ],
        compiler_params=pltpu.CompilerParams(
            collective_id=0, has_side_effects=True, vmem_limit_bytes=40 * 1024 * 1024
        ),
    )(
        right_side.reshape(field),
        batch_order.reshape(1, COLS),
        light_diag.reshape(block),
        light_hops.reshape(hops),
        charm_diag.reshape(block),
        charm_hops.reshape(hops),
        current_blocks.reshape(block),
    )
    shape = (1, 1, LX, LY, NC, 2 * COLS)
    return light.reshape(shape), seq.reshape(shape), margin


def solution(mesh):
    site = P("tm", "space", None, None, None, None)
    hop = P(None, "tm", "space", None, None, None, None)
    return jax.shard_map(
        body,
        mesh=mesh,
        in_specs=(site, P(), site, hop, site, hop, site),
        out_specs=(site, site, P()),
        check_vma=False,
    )
```

profile of v0, /device:TPU:32, one launch (start us, length us, event | category | flops | bytes accessed | tf_op | source)
XLA Modules:
  0.0 73.7 jit_solution(3822493005039461704)
XLA Ops:
  0.6 0.0 copy-start
  0.6 1.6 %copy-done = bf16[8,1,1,4,4,64,128]{6,5,4,3,2,1,0:T(8,128)(2,1)S(1)} copy-done((bf16[8,1,1,4,4,64,128]{6,5,4,3,2,1,0:T(8,128)(2,1)S(1)}, bf16[8,1,1,4,4,64,128]{6,5,4,3,2,1,0:T(8,128)(2,1)}, u32[]{:S(2)}) %copy-start) | copy-done | bytes 2097176
  2.2 0.0 copy-start.1
  2.2 1.6 %copy-done.1 = bf16[8,1,1,4,4,64,128]{6,5,4,3,2,1,0:T(8,128)(2,1)S(1)} copy-done((bf16[8,1,1,4,4,64,128]{6,5,4,3,2,1,0:T(8,128)(2,1)S(1)}, bf16[8,1,1,4,4,64,128]{6,5,4,3,2,1,0:T(8,128)(2,1)}, u32[]{:S(2)}) %copy-start.1) | copy-done | bytes 2097176
  3.8 0.0 copy-start.2
  3.8 0.9 %copy-done.2 = bf16[1,1,4,4,64,64]{5,4,3,2,1,0:T(8,128)(2,1)S(1)} copy-done((bf16[1,1,4,4,64,64]{5,4,3,2,1,0:T(8,128)(2,1)S(1)}, bf16[1,1,4,4,64,64]{5,4,3,2,1,0:T(8,128)(2,1)}, u32[]{:S(2)}) %copy-start.2) | copy-done | bytes 131096
  4.8 0.0 copy-start.3
  4.8 0.9 %copy-done.3 = bf16[1,1,4,4,64,128]{5,4,3,2,1,0:T(8,128)(2,1)S(1)} copy-done((bf16[1,1,4,4,64,128]{5,4,3,2,1,0:T(8,128)(2,1)S(1)}, bf16[1,1,4,4,64,128]{5,4,3,2,1,0:T(8,128)(2,1)}, u32[]{:S(2)}) %copy-start.3) | copy-done | bytes 262168
  5.7 0.0 copy-start.4
  5.7 0.9 %copy-done.4 = bf16[1,1,4,4,64,128]{5,4,3,2,1,0:T(8,128)(2,1)S(1)} copy-done((bf16[1,1,4,4,64,128]{5,4,3,2,1,0:T(8,128)(2,1)S(1)}, bf16[1,1,4,4,64,128]{5,4,3,2,1,0:T(8,128)(2,1)}, u32[]{:S(2)}) %copy-start.4) | copy-done | bytes 262168
  6.7 0.0 copy-start.5
  6.7 0.9 %copy-done.5 = bf16[1,1,4,4,64,128]{5,4,3,2,1,0:T(8,128)(2,1)S(1)} copy-done((bf16[1,1,4,4,64,128]{5,4,3,2,1,0:T(8,128)(2,1)S(1)}, bf16[1,1,4,4,64,128]{5,4,3,2,1,0:T(8,128)(2,1)}, u32[]{:S(2)}) %copy-start.5) | copy-done | bytes 262168
  7.6 0.0 copy-start.6
  7.6 0.7 copy-done.6
  8.3 63.4 %shard_map.94 = (bf16[16,64,64]{2,1,0:T(8,128)(2,1)S(1)}, bf16[16,64,64]{2,1,0:T(8,128)(2,1)S(1)}, f32[2,32,32]{2,1,0:T(8,128)S(1)}) custom-call(bf16[16,64,64]{2,1,0:T(8,128)(2,1)S(1)} %bitcast.13, s32[1,32]{1,0:T(1,128)S(1)} %bitcast.17, bf16[16,64,128]{2,1,0:T(8,128)(2,1)S(1)} %bitcast.14, bf16[8,16,64,128]{3,2,1,0:T(8,128)(2,1)S(1)} %bitcast.9, ...), custom_call_target="tpu_custom_call" | custom-call | tf_op jit(solution)/shard_map/pallas_call | solution.py:322
  71.6 0.7 copy.13
  72.3 0.7 copy.14
  73.0 0.6 copy.15
Async XLA Ops:
  0.6 1.6 %copy-start = (bf16[8,1,1,4,4,64,128]{6,5,4,3,2,1,0:T(8,128)(2,1)S(1)}, bf16[8,1,1,4,4,64,128]{6,5,4,3,2,1,0:T(8,128)(2,1)}, u32[]{:S(2)}) copy-start(bf16[8,1,1,4,4,64,128]{6,5,4,3,2,1,0:T(8,128)(2,1)} %param.10) | copy-start | bytes 6291460
  2.2 1.6 %copy-start.1 = (bf16[8,1,1,4,4,64,128]{6,5,4,3,2,1,0:T(8,128)(2,1)S(1)}, bf16[8,1,1,4,4,64,128]{6,5,4,3,2,1,0:T(8,128)(2,1)}, u32[]{:S(2)}) copy-start(bf16[8,1,1,4,4,64,128]{6,5,4,3,2,1,0:T(8,128)(2,1)} %param.12) | copy-start | bytes 6291460
  3.8 0.9 %copy-start.2 = (bf16[1,1,4,4,64,64]{5,4,3,2,1,0:T(8,128)(2,1)S(1)}, bf16[1,1,4,4,64,64]{5,4,3,2,1,0:T(8,128)(2,1)}, u32[]{:S(2)}) copy-start(bf16[1,1,4,4,64,64]{5,4,3,2,1,0:T(8,128)(2,1)} %param.7) | copy-start | bytes 393220
  4.8 0.9 %copy-start.3 = (bf16[1,1,4,4,64,128]{5,4,3,2,1,0:T(8,128)(2,1)S(1)}, bf16[1,1,4,4,64,128]{5,4,3,2,1,0:T(8,128)(2,1)}, u32[]{:S(2)}) copy-start(bf16[1,1,4,4,64,128]{5,4,3,2,1,0:T(8,128)(2,1)} %param.9) | copy-start | bytes 786436
  5.7 0.9 %copy-start.4 = (bf16[1,1,4,4,64,128]{5,4,3,2,1,0:T(8,128)(2,1)S(1)}, bf16[1,1,4,4,64,128]{5,4,3,2,1,0:T(8,128)(2,1)}, u32[]{:S(2)}) copy-start(bf16[1,1,4,4,64,128]{5,4,3,2,1,0:T(8,128)(2,1)} %param.11) | copy-start | bytes 786436
  6.7 0.9 %copy-start.5 = (bf16[1,1,4,4,64,128]{5,4,3,2,1,0:T(8,128)(2,1)S(1)}, bf16[1,1,4,4,64,128]{5,4,3,2,1,0:T(8,128)(2,1)}, u32[]{:S(2)}) copy-start(bf16[1,1,4,4,64,128]{5,4,3,2,1,0:T(8,128)(2,1)} %param.13) | copy-start | bytes 786436
  7.6 0.7 copy-start.6
where the time goes:
time: 73.9 us; the launch traced here: 73.7 us
  Pallas kernels  63.4 us (86%)
  local copies, waits for them, and re-layouts  9.65 us (13%)
    pallas_call x1, Pallas kernels, body(): pl.pallas_call(body_kernel, out_shape=(jax.ShapeDtypeStruct(field, BF), j...  63.4 us
    unnamed x17, local copies, waits for them, and re-layouts  9.65 us

commit v1 on v0

--- a/solution.py
+++ b/solution.py
@@ -37,11 +37,11 @@
 
 
 def body_kernel(
-    right_hbm, order_ref, ldiag_hbm, lhops_hbm, cdiag_hbm, chops_hbm, current_hbm,
+    right_hbm, order_hbm, ldiag_hbm, lhops_hbm, cdiag_hbm, chops_hbm, current_hbm,
     light_out, seq_out, margin_ref,
-    right, ldiag, lhops, cdiag, chops, current,
-    sent, halo, local, base, acc, light_t, light_v, seq_v, red,
-    in_sem, out_sem, send_sem, recv_sem, red_send, red_recv,
+    right, order_ref, ldiag, lhops, cdiag, chops, current,
+    sent, halo, local, base, acc, light_t, red,
+    in_sem, send_sem, recv_sem, red_send, red_recv,
 ):
     space = lax.axis_index("space")
     tm = lax.axis_index("tm")
@@ -82,9 +82,10 @@
             (cdiag_hbm, cdiag),
             (chops_hbm.at[pl.ds(0, 4)], chops.at[pl.ds(0, 4)]),
             (chops_hbm.at[pl.ds(4, 4)], chops.at[pl.ds(4, 4)]),
+            (order_hbm, order_ref),
         ))
     ]
-    for copy in loads:
+    for copy in loads[-1:] + loads[:-1]:
         copy.start()
 
     barrier = pltpu.get_barrier_semaphore()
@@ -117,19 +118,15 @@
         return jnp.concatenate([pair_blocks(ref.at[e], pair) for e in numbers], axis=1)
 
     def on_site(ref, pair, field32):
-        v32 = field32.astype(BF).astype(F32)
-        widened = jnp.concatenate([v32.astype(BF), turn(v32).astype(BF)], axis=0)
-        return product(pair_blocks(ref, pair), widened)
+        v = field32.astype(BF)
+        return product(pair_blocks(ref, pair), jnp.concatenate([v, turn(v)], axis=0))
 
     def keep(round_, pair, field32):
-        v32 = field32.astype(BF).astype(F32)
-        v = v32.astype(BF)
+        v = field32.astype(BF)
         sent[round_, pair] = v
-        swapped = swap(v32)
-        local[pair, 0] = jnp.concatenate([v, turn(v32).astype(BF)], axis=0)
-        local[pair, 1] = jnp.concatenate(
-            [swapped.astype(BF), turn(swapped).astype(BF)], axis=0
-        )
+        swapped = swap(v)
+        local[pair, 0] = jnp.concatenate([v, turn(v)], axis=0)
+        local[pair, 1] = jnp.concatenate([swapped, turn(swapped)], axis=0)
 
     def halo_copy(round_, direction, chunk):
         part = pl.ds(chunk * PER, PER)
@@ -163,7 +160,7 @@
         parts = []
         for direction in range(4):
             v = halo[round_, direction, pair]
-            parts += [v, turn(v.astype(F32)).astype(BF)]
+            parts += [v, turn(v)]
         residue = acc[pair] + product(
             hop_blocks(hops, pair, (4, 5, 6, 7)), jnp.concatenate(parts, axis=0)
         )
@@ -176,13 +173,13 @@
     def pairs_of(chunk):
         return range(chunk * PER, (chunk + 1) * PER)
 
+    loads[8].wait()
     order = jnp.concatenate([order_ref[...]] * 4, axis=1)
     picked = order + jnp.where(low[:1], 0, COLS)
     row = lax.broadcasted_iota(jnp.int32, (2 * COLS, LANES), 0)
     hit = row == picked
     pick_one = jnp.where(jnp.logical_and(hit, first), 1.0, 0.0).astype(BF)
     pick_two = jnp.where(jnp.logical_and(hit, jnp.logical_not(first)), 1.0, 0.0).astype(BF)
-    pick = jnp.concatenate([pick_one, pick_two], axis=0)
 
     loads[0].wait()
     loads[1].wait()
@@ -238,9 +235,7 @@
     loads[6].wait()
     loads[7].wait()
     for pair in range(PAIRS):
-        put(light_v, pair, light_t[pair])
-    light_copy = pltpu.make_async_copy(light_v, light_out, out_sem.at[0])
-    light_copy.start()
+        put(light_out, pair, light_t[pair])
 
     def charm_sweep(step, carry):
         local_phase(chops)
@@ -262,9 +257,7 @@
             gram = gram + lax.dot_general(
                 light_t[pair], v, (((0,), (0,)), ((), ())), preferred_element_type=F32
             )
-            put(seq_v, pair, v)
-    seq_copy = pltpu.make_async_copy(seq_v, seq_out, out_sem.at[1])
-    seq_copy.start()
+            put(seq_out, pair, v)
 
     upper = gram[:COLS] + pltpu.roll(gram[COLS:2 * COLS], 3 * COLS, axis=1)
     lower = pltpu.roll(gram[2 * COLS:3 * COLS], 2 * COLS, axis=1) + pltpu.roll(
@@ -304,12 +297,27 @@
     margin_ref[1, :half] = total[:, 2 * COLS:3 * COLS]
     margin_ref[1, half:] = total[:, 3 * COLS:]
 
-    light_copy.wait()
-    seq_copy.wait()
     for round_ in range(ROUNDS):
         for chunk in range(CHUNKS):
             for direction in range(4):
                 halo_copy(round_, direction, chunk).wait_send()
+
+
+def finish_kernel(light_in, seq_in, margin_in, light_out, seq_out, margin_out, sem):
+    copies = [
+        pltpu.make_async_copy(src, dst, sem.at[i])
+        for i, (src, dst) in enumerate(
+            ((light_in, light_out), (seq_in, seq_out), (margin_in, margin_out))
+        )
+    ]
+    for copy in copies:
+        copy.start()
+    for copy in copies:
+        copy.wait()
+
+
+def stay(array):
+    return pltpu.with_memory_space_constraint(array, pltpu.HBM)
 
 
 def body(right_side, batch_order, light_diag, light_hops, charm_diag, charm_hops, current_blocks):
@@ -326,10 +334,11 @@
             jax.ShapeDtypeStruct(field, BF),
             jax.ShapeDtypeStruct((2, COLS, COLS), F32),
         ),
-        in_specs=[anywhere, vmem, anywhere, anywhere, anywhere, anywhere, anywhere],
-        out_specs=(anywhere, anywhere, vmem),
+        in_specs=[anywhere, anywhere, anywhere, anywhere, anywhere, anywhere, anywhere],
+        out_specs=(vmem, vmem, vmem),
         scratch_shapes=[
             pltpu.VMEM(field, BF),
+            pltpu.VMEM((1, COLS), jnp.int32),
             pltpu.VMEM(block, BF),
             pltpu.VMEM(hops, BF),
             pltpu.VMEM(block, BF),
@@ -341,28 +350,37 @@
             pltpu.VMEM((PAIRS,) + packed, BF),
             pltpu.VMEM((PAIRS,) + packed, F32),
             pltpu.VMEM((PAIRS,) + packed, BF),
-            pltpu.VMEM(field, BF),
-            pltpu.VMEM(field, BF),
             pltpu.VMEM((SLOTS, COLS // 2, LANES), F32),
-            pltpu.SemaphoreType.DMA((8,)),
-            pltpu.SemaphoreType.DMA((2,)),
+            pltpu.SemaphoreType.DMA((9,)),
             pltpu.SemaphoreType.DMA((ROUNDS, 4, CHUNKS)),
             pltpu.SemaphoreType.DMA((ROUNDS, 4, CHUNKS)),
             pltpu.SemaphoreType.DMA((SLOTS,)),
             pltpu.SemaphoreType.DMA((SLOTS,)),
         ],
         compiler_params=pltpu.CompilerParams(
-            collective_id=0, has_side_effects=True, vmem_limit_bytes=40 * 1024 * 1024
+            collective_id=0, has_side_effects=True, vmem_limit_bytes=32 * 1024 * 1024
         ),
     )(
-        right_side.reshape(field),
-        batch_order.reshape(1, COLS),
-        light_diag.reshape(block),
-        light_hops.reshape(hops),
-        charm_diag.reshape(block),
-        charm_hops.reshape(hops),
-        current_blocks.reshape(block),
-    )
+        stay(right_side.reshape(field)),
+        stay(batch_order.reshape(1, COLS)),
+        stay(light_diag.reshape(block)),
+        stay(light_hops.reshape(hops)),
+        stay(charm_diag.reshape(block)),
+        stay(charm_hops.reshape(hops)),
+        stay(current_blocks.reshape(block)),
+    )
+    light, seq, margin = pl.pallas_call(
+        finish_kernel,
+        out_shape=(
+            jax.ShapeDtypeStruct(field, BF),
+            jax.ShapeDtypeStruct(field, BF),
+            jax.ShapeDtypeStruct((2, COLS, COLS), F32),
+        ),
+        in_specs=[anywhere] * 3,
+        out_specs=(anywhere,) * 3,
+        scratch_shapes=[pltpu.SemaphoreType.DMA((3,))],
+        compiler_params=pltpu.CompilerParams(vmem_limit_bytes=1024 * 1024),
+    )(light, seq, margin)
     shape = (1, 1, LX, LY, NC, 2 * COLS)
     return light.reshape(shape), seq.reshape(shape), margin
 

time: 73.9 us -> 64.5 us (0.87)
  local copies, waits for them, and re-layouts: 9.65 us -> 0 us
    unnamed x17 -> x0, local copies, waits for them, and re-layouts: 9.65 us -> none
    pallas_call x0 -> x1, Pallas kernels: none -> 0.82 us  [body(): pl.pallas_call(finish_kernel, out_shape=(jax.ShapeDtypeStruct(field, BF),...]
where the time goes in v1:
time: 64.5 us
  Pallas kernels  63.8 us (99%)
    pallas_call x1, Pallas kernels, body(): pl.pallas_call(body_kernel, out_shape=(jax.ShapeDtypeStruct(field, BF), j...  63 us

profile of v1, /device:TPU:32, one launch (start us, length us, event | category | flops | bytes accessed | tf_op | source)
XLA Modules:
  0.0 64.5 jit_solution(15714131706292052999)
XLA Ops:
  0.6 63.0 %shard_map.94 = (bf16[16,64,64]{2,1,0:T(8,128)(2,1)S(1)}, bf16[16,64,64]{2,1,0:T(8,128)(2,1)S(1)}, f32[2,32,32]{2,1,0:T(8,128)S(1)}) custom-call(bf16[16,64,64]{2,1,0:T(8,128)(2,1)} %bitcast.11, s32[1,32]{1,0:T(1,128)} %bitcast.15, bf16[16,64,128]{2,1,0:T(8,128)(2,1)} %bitcast.12, bf16[8,16,64,128]{3,2,1,0:T(8,128)(2,1)} %bitcast.9, ...), custom_call_target="tpu_custom_call" | custom-call | tf_op jit(solution)/shard_map/pallas_call | solution.py:330
  63.6 0.8 %shard_map.95 = (bf16[16,64,64]{2,1,0:T(8,128)(2,1)}, bf16[16,64,64]{2,1,0:T(8,128)(2,1)}, f32[2,32,32]{2,1,0:T(8,128)}) custom-call(bf16[16,64,64]{2,1,0:T(8,128)(2,1)S(1)} %get-tuple-element.9.light_in, bf16[16,64,64]{2,1,0:T(8,128)(2,1)S(1)} %get-tuple-element.10.seq_in, f32[2,32,32]{2,1,0:T(8,128)S(1)} %get-tuple-element.11.margin_in), custom_call_target="tpu_custom_call" | custom-call | tf_op jit(solution)/shard_map/pallas_call | solution.py:372

commit v2 on v1

--- a/solution.py
+++ b/solution.py
@@ -41,6 +41,7 @@
     light_out, seq_out, margin_ref,
     right, order_ref, ldiag, lhops, cdiag, chops, current,
     sent, halo, local, base, acc, light_t, red,
+    weight, gram_ref, pull, pull_sent, pull_halo, pull_send, pull_recv,
     in_sem, send_sem, recv_sem, red_send, red_recv,
 ):
     space = lax.axis_index("space")
@@ -246,18 +247,89 @@
             send(step + 1, chunk)
         return carry
 
+    def site_rows(v, which):
+        one = which * COLS
+        return jnp.concatenate(
+            [v[one:one + COLS], v[2 * COLS + one:3 * COLS + one]], axis=0
+        )
+
+    def adjoint(rows, blocks, high):
+        out = jnp.dot(rows, blocks, preferred_element_type=F32)
+        rolled = pltpu.roll(out, NC, axis=1)
+        if high:
+            return rolled[:COLS] + out[COLS:], rolled[COLS:] - out[:COLS]
+        return out[:COLS] + rolled[COLS:], out[COLS:] - rolled[:COLS]
+
+    def stack(one, two):
+        return jnp.concatenate([one[0], two[0], one[1], two[1]], axis=0)
+
+    low_tall = lax.broadcasted_iota(jnp.int32, (LANES, LANES), 1) < NC
+
+    gram_ref[...] = jnp.zeros((LANES, LANES), F32)
+
+    def weigh(px, carry):
+        for h in range(2):
+            across = jnp.transpose(light_t[px * 2 + h], (1, 0))
+            halves = []
+            for which in range(2):
+                site = px * LY + h + 2 * which
+                real, imag = adjoint(site_rows(across, which), cdiag[site], False)
+                weight[site] = jnp.concatenate([real, imag], axis=0)[:, :NC].astype(BF)
+                halves.append((real[:, :NC], imag[:, :NC]))
+            gram_ref[...] += jnp.dot(
+                stack(*halves).astype(BF), base[px * 2 + h], preferred_element_type=F32
+            )
+        return carry
+
+    def plane(e, px, h_low, swap_low, swap_high):
+        sides = []
+        for high, h, swapped in ((False, h_low, swap_low), (True, 1 - h_low, swap_high)):
+            both = [
+                adjoint(weight[px * LY + h + 2 * i], chops[e, px * LY + h + 2 * i], high)
+                for i in range(2)
+            ]
+            sides.append(stack(both[1], both[0]) if swapped else stack(both[0], both[1]))
+        return jnp.where(low_tall, sides[0], sides[1])
+
+    def weigh_remote(px, carry):
+        for direction in range(4):
+            pull_sent[direction, px] = plane(4 + direction, px, 0, False, False).astype(BF)
+        return carry
+
+    def pull_copy(direction):
+        return pltpu.make_async_remote_copy(
+            src_ref=pull_sent.at[direction],
+            dst_ref=pull_halo.at[direction],
+            send_sem=pull_send.at[direction],
+            recv_sem=pull_recv.at[direction],
+            device_id=takers[direction ^ 1],
+            device_id_type=MESH,
+        )
+
+    def weigh_local(px, carry):
+        pull[lax.rem(px + 1, LX)] += plane(0, px, 0, False, False)
+        pull[lax.rem(px + LX - 1, LX)] += plane(1, px, 0, False, False)
+        pull[px] += plane(2, px, 1, True, False) + plane(3, px, 1, False, True)
+        return carry
+
+    lax.fori_loop(0, LX, weigh, 0)
+    lax.fori_loop(0, LX, weigh_remote, 0)
+    for direction in range(4):
+        pull_copy(direction).start()
+    pull[...] = jnp.zeros((LX, LANES, LANES), F32)
+    lax.fori_loop(0, LX, weigh_local, 0)
+
     lax.fori_loop(3, 5, charm_sweep, 0)
 
-    local_phase(chops)
-    gram = jnp.zeros((LANES, LANES), F32)
-    for chunk in range(CHUNKS):
-        arrive(5, chunk)
-        for pair in pairs_of(chunk):
-            v = remote_pair(5, chops, cdiag, pair).astype(BF)
-            gram = gram + lax.dot_general(
-                light_t[pair], v, (((0,), (0,)), ((), ())), preferred_element_type=F32
-            )
-            put(seq_out, pair, v)
+    for direction in range(4):
+        pull_copy(direction).wait_recv()
+    gram = gram_ref[...]
+    for px in range(LX):
+        pulled = pull[px]
+        for direction in range(4):
+            pulled = pulled + pull_halo[direction, px].astype(F32)
+        field = jnp.concatenate([sent[5, px * 2], sent[5, px * 2 + 1]], axis=0)
+        gram = gram + jnp.dot(pulled.astype(BF), field, preferred_element_type=F32)
 
     upper = gram[:COLS] + pltpu.roll(gram[COLS:2 * COLS], 3 * COLS, axis=1)
     lower = pltpu.roll(gram[2 * COLS:3 * COLS], 2 * COLS, axis=1) + pltpu.roll(
@@ -270,33 +342,57 @@
     )
 
     mine = (core, y, x, z)
-    for stage, (count, offset) in enumerate(STAGES):
-        me = mine[stage]
-        red[offset + me] = total
-        copies = []
+
+    def reduce_copy(stage, step):
+        slot = STAGES[stage][1] + mine[stage]
+        return pltpu.make_async_remote_copy(
+            src_ref=red.at[slot],
+            dst_ref=red.at[slot],
+            send_sem=red_send.at[STAGES[stage][1] + step],
+            recv_sem=red_recv.at[STAGES[stage][1] + step],
+            device_id=partner(stage, step),
+            device_id_type=MESH,
+        )
+
+    def reduce_start(stage, total):
+        count, offset = STAGES[stage]
+        red[offset + mine[stage]] = total
         for step in range(1, count):
-            copies.append(pltpu.make_async_remote_copy(
-                src_ref=red.at[offset + me],
-                dst_ref=red.at[offset + me],
-                send_sem=red_send.at[offset + step],
-                recv_sem=red_recv.at[offset + step],
-                device_id=partner(stage, step),
-                device_id_type=MESH,
-            ))
-        for copy in copies:
-            copy.start()
-        for copy in copies:
-            copy.wait()
+            reduce_copy(stage, step).start()
+
+    def reduce_done(stage):
+        count, offset = STAGES[stage]
+        for step in range(1, count):
+            reduce_copy(stage, step).wait_recv()
         total = red[offset]
         for slot in range(1, count):
             total = total + red[offset + slot]
-
+        return total
+
+    def last_chunk(chunk):
+        arrive(5, chunk)
+        for pair in pairs_of(chunk):
+            put(seq_out, pair, remote_pair(5, chops, cdiag, pair).astype(BF))
+
+    reduce_start(0, total)
+    local_phase(chops)
+    reduce_start(1, reduce_done(0))
+    reduce_start(2, reduce_done(1))
+    for chunk in range(CHUNKS):
+        last_chunk(chunk)
+    reduce_start(3, reduce_done(2))
+    total = reduce_done(3)
     total = total * (1.0 / math.sqrt(n_space * n_tm * SITES * NC))
     margin_ref[0, :half] = total[:, :COLS]
     margin_ref[0, half:] = total[:, COLS:2 * COLS]
     margin_ref[1, :half] = total[:, 2 * COLS:3 * COLS]
     margin_ref[1, half:] = total[:, 3 * COLS:]
 
+    for direction in range(4):
+        pull_copy(direction).wait_send()
+    for stage, (count, _) in enumerate(STAGES):
+        for step in range(1, count):
+            reduce_copy(stage, step).wait_send()
     for round_ in range(ROUNDS):
         for chunk in range(CHUNKS):
             for direction in range(4):
@@ -351,6 +447,13 @@
             pltpu.VMEM((PAIRS,) + packed, F32),
             pltpu.VMEM((PAIRS,) + packed, BF),
             pltpu.VMEM((SLOTS, COLS // 2, LANES), F32),
+            pltpu.VMEM((SITES, 2 * COLS, NC), BF),
+            pltpu.VMEM((LANES, LANES), F32),
+            pltpu.VMEM((LX, LANES, LANES), F32),
+            pltpu.VMEM((4, LX, LANES, LANES), BF),
+            pltpu.VMEM((4, LX, LANES, LANES), BF),
+            pltpu.SemaphoreType.DMA((4,)),
+            pltpu.SemaphoreType.DMA((4,)),
             pltpu.SemaphoreType.DMA((9,)),
             pltpu.SemaphoreType.DMA((ROUNDS, 4, CHUNKS)),
             pltpu.SemaphoreType.DMA((ROUNDS, 4, CHUNKS)),

time: 64.5 us -> 63.5 us (0.984)
  Pallas kernels: 63.8 us -> 62.8 us
    pallas_call x1, Pallas kernels: 63 us -> 62 us  [body(): pl.pallas_call(body_kernel, out_shape=(jax.ShapeDtypeStruct(field, BF), j...]
where the time goes in v2:
time: 63.5 us; the launch traced here: 63.4 us
  Pallas kernels  62.8 us (99%)
  between operations  0.64 us (1%)
    pallas_call x1, Pallas kernels, body(): pl.pallas_call(body_kernel, out_shape=(jax.ShapeDtypeStruct(field, BF), j...  62 us

profile of v2, /device:TPU:32, one launch (start us, length us, event | category | flops | bytes accessed | tf_op | source)
XLA Modules:
  0.0 63.4 jit_solution(5381705638983896011)
XLA Ops:
  0.6 62.0 %shard_map.94 = (bf16[16,64,64]{2,1,0:T(8,128)(2,1)S(1)}, bf16[16,64,64]{2,1,0:T(8,128)(2,1)S(1)}, f32[2,32,32]{2,1,0:T(8,128)S(1)}) custom-call(bf16[16,64,64]{2,1,0:T(8,128)(2,1)} %bitcast.11, s32[1,32]{1,0:T(1,128)} %bitcast.15, bf16[16,64,128]{2,1,0:T(8,128)(2,1)} %bitcast.12, bf16[8,16,64,128]{3,2,1,0:T(8,128)(2,1)} %bitcast.9, ...), custom_call_target="tpu_custom_call" | custom-call | tf_op jit(solution)/shard_map/pallas_call | solution.py:426
  62.6 0.8 %shard_map.95 = (bf16[16,64,64]{2,1,0:T(8,128)(2,1)}, bf16[16,64,64]{2,1,0:T(8,128)(2,1)}, f32[2,32,32]{2,1,0:T(8,128)}) custom-call(bf16[16,64,64]{2,1,0:T(8,128)(2,1)S(1)} %get-tuple-element.9.light_in, bf16[16,64,64]{2,1,0:T(8,128)(2,1)S(1)} %get-tuple-element.10.seq_in, f32[2,32,32]{2,1,0:T(8,128)S(1)} %get-tuple-element.11.margin_in), custom_call_target="tpu_custom_call" | custom-call | tf_op jit(solution)/shard_map/pallas_call | solution.py:475

commit v3 on v2

--- a/solution.py
+++ b/solution.py
@@ -27,8 +27,8 @@
 Z = 8
 CORES = 2
 X = 4
-STAGES = ((CORES, 0), (Y, 2), (X, 6), (Z, 10))
-SLOTS = 18
+STAGES = ((Y * CORES, 0), (X, 8), (Z, 12))
+SLOTS = 20
 
 
 def sites_of(pair):
@@ -58,10 +58,9 @@
 
     def partner(stage, step):
         if stage == 0:
-            return device(x, y, z, lax.rem(core + step, CORES))
+            row = lax.rem(y * CORES + core + step, Y * CORES)
+            return device(x, row // CORES, z, lax.rem(row, CORES))
         if stage == 1:
-            return device(x, lax.rem(y + step, Y), z, core)
-        if stage == 2:
             return device(lax.rem(x + step, X), y, z, core)
         return device(x, y, lax.rem(z + step, Z), core)
 
@@ -193,7 +192,7 @@
             base[pair] = both.astype(BF)
             keep(0, pair, on_site(ldiag, pair, both))
         if chunk == 0:
-            pl.semaphore_wait(barrier, SLOTS)
+            pl.semaphore_wait(barrier, len(greeted))
         send(0, chunk)
     loads[2].wait()
     loads[3].wait()
@@ -341,7 +340,7 @@
         first[:half], sums[:half], pltpu.roll(sums[half:], COLS, axis=1)
     )
 
-    mine = (core, y, x, z)
+    mine = (y * CORES + core, x, z)
 
     def reduce_copy(stage, step):
         slot = STAGES[stage][1] + mine[stage]
@@ -377,11 +376,12 @@
     reduce_start(0, total)
     local_phase(chops)
     reduce_start(1, reduce_done(0))
+    for chunk in range(2):
+        last_chunk(chunk)
     reduce_start(2, reduce_done(1))
-    for chunk in range(CHUNKS):
+    for chunk in range(2, CHUNKS):
         last_chunk(chunk)
-    reduce_start(3, reduce_done(2))
-    total = reduce_done(3)
+    total = reduce_done(2)
     total = total * (1.0 / math.sqrt(n_space * n_tm * SITES * NC))
     margin_ref[0, :half] = total[:, :COLS]
     margin_ref[0, half:] = total[:, COLS:2 * COLS]

time: 63.5 us -> 62.4 us (0.983)
  Pallas kernels: 62.8 us -> 61.4 us
    pallas_call x1, Pallas kernels: 62 us -> 60.6 us  [body(): pl.pallas_call(body_kernel, out_shape=(jax.ShapeDtypeStruct(field, BF), j...]
where the time goes in v3:
time: 62.4 us; the launch traced here: 62 us
  Pallas kernels  61.4 us (98%)
  between operations  0.64 us (1%)
    pallas_call x1, Pallas kernels, body(): pl.pallas_call(body_kernel, out_shape=(jax.ShapeDtypeStruct(field, BF), j...  60.6 us

profile of v3, /device:TPU:32, one launch (start us, length us, event | category | flops | bytes accessed | tf_op | source)
XLA Modules:
  0.0 62.0 jit_solution(4566742221089194939)
XLA Ops:
  0.6 60.6 %shard_map.94 = (bf16[16,64,64]{2,1,0:T(8,128)(2,1)S(1)}, bf16[16,64,64]{2,1,0:T(8,128)(2,1)S(1)}, f32[2,32,32]{2,1,0:T(8,128)S(1)}) custom-call(bf16[16,64,64]{2,1,0:T(8,128)(2,1)} %bitcast.11, s32[1,32]{1,0:T(1,128)} %bitcast.15, bf16[16,64,128]{2,1,0:T(8,128)(2,1)} %bitcast.12, bf16[8,16,64,128]{3,2,1,0:T(8,128)(2,1)} %bitcast.9, ...), custom_call_target="tpu_custom_call" | custom-call | tf_op jit(solution)/shard_map/pallas_call | solution.py:426
  61.2 0.8 %shard_map.95 = (bf16[16,64,64]{2,1,0:T(8,128)(2,1)}, bf16[16,64,64]{2,1,0:T(8,128)(2,1)}, f32[2,32,32]{2,1,0:T(8,128)}) custom-call(bf16[16,64,64]{2,1,0:T(8,128)(2,1)S(1)} %get-tuple-element.9.light_in, bf16[16,64,64]{2,1,0:T(8,128)(2,1)S(1)} %get-tuple-element.10.seq_in, f32[2,32,32]{2,1,0:T(8,128)S(1)} %get-tuple-element.11.margin_in), custom_call_target="tpu_custom_call" | custom-call | tf_op jit(solution)/shard_map/pallas_call | solution.py:475

commit v4 on v3

--- a/solution.py
+++ b/solution.py
@@ -234,8 +234,6 @@
         send(3, chunk)
     loads[6].wait()
     loads[7].wait()
-    for pair in range(PAIRS):
-        put(light_out, pair, light_t[pair])
 
     def charm_sweep(step, carry):
         local_phase(chops)
@@ -290,11 +288,6 @@
             sides.append(stack(both[1], both[0]) if swapped else stack(both[0], both[1]))
         return jnp.where(low_tall, sides[0], sides[1])
 
-    def weigh_remote(px, carry):
-        for direction in range(4):
-            pull_sent[direction, px] = plane(4 + direction, px, 0, False, False).astype(BF)
-        return carry
-
     def pull_copy(direction):
         return pltpu.make_async_remote_copy(
             src_ref=pull_sent.at[direction],
@@ -311,9 +304,11 @@
         pull[px] += plane(2, px, 1, True, False) + plane(3, px, 1, False, True)
         return carry
 
-    lax.fori_loop(0, LX, weigh, 0)
-    lax.fori_loop(0, LX, weigh_remote, 0)
+    for px in range(LX):
+        weigh(px, 0)
     for direction in range(4):
+        for px in range(LX):
+            pull_sent[direction, px] = plane(4 + direction, px, 0, False, False).astype(BF)
         pull_copy(direction).start()
     pull[...] = jnp.zeros((LX, LANES, LANES), F32)
     lax.fori_loop(0, LX, weigh_local, 0)
@@ -381,6 +376,8 @@
     reduce_start(2, reduce_done(1))
     for chunk in range(2, CHUNKS):
         last_chunk(chunk)
+    for pair in range(PAIRS):
+        put(light_out, pair, light_t[pair])
     total = reduce_done(2)
     total = total * (1.0 / math.sqrt(n_space * n_tm * SITES * NC))
     margin_ref[0, :half] = total[:, :COLS]

time: 62.4 us -> 60.6 us (0.971)
  Pallas kernels: 61.4 us -> 59.5 us
    pallas_call x1, Pallas kernels: 60.6 us -> 58.7 us  [body(): pl.pallas_call(body_kernel, out_shape=(jax.ShapeDtypeStruct(field, BF), j...]
where the time goes in v4:
time: 60.6 us; the launch traced here: 60.2 us
  Pallas kernels  59.5 us (98%)
  between operations  0.64 us (1%)
    pallas_call x1, Pallas kernels, body(): pl.pallas_call(body_kernel, out_shape=(jax.ShapeDtypeStruct(field, BF), j...  58.7 us

profile of v4, /device:TPU:32, one launch (start us, length us, event | category | flops | bytes accessed | tf_op | source)
XLA Modules:
  0.0 60.2 jit_solution(17897874346153026080)
XLA Ops:
  0.6 58.7 %shard_map.94 = (bf16[16,64,64]{2,1,0:T(8,128)(2,1)S(1)}, bf16[16,64,64]{2,1,0:T(8,128)(2,1)S(1)}, f32[2,32,32]{2,1,0:T(8,128)S(1)}) custom-call(bf16[16,64,64]{2,1,0:T(8,128)(2,1)} %bitcast.11, s32[1,32]{1,0:T(1,128)} %bitcast.15, bf16[16,64,128]{2,1,0:T(8,128)(2,1)} %bitcast.12, bf16[8,16,64,128]{3,2,1,0:T(8,128)(2,1)} %bitcast.9, ...), custom_call_target="tpu_custom_call" | custom-call | tf_op jit(solution)/shard_map/pallas_call | solution.py:423
  59.3 0.8 %shard_map.95 = (bf16[16,64,64]{2,1,0:T(8,128)(2,1)}, bf16[16,64,64]{2,1,0:T(8,128)(2,1)}, f32[2,32,32]{2,1,0:T(8,128)}) custom-call(bf16[16,64,64]{2,1,0:T(8,128)(2,1)S(1)} %get-tuple-element.9.light_in, bf16[16,64,64]{2,1,0:T(8,128)(2,1)S(1)} %get-tuple-element.10.seq_in, f32[2,32,32]{2,1,0:T(8,128)S(1)} %get-tuple-element.11.margin_in), custom_call_target="tpu_custom_call" | custom-call | tf_op jit(solution)/shard_map/pallas_call | solution.py:472

commit v5 on v4

--- a/solution.py
+++ b/solution.py
@@ -191,8 +191,8 @@
             )
             base[pair] = both.astype(BF)
             keep(0, pair, on_site(ldiag, pair, both))
-        if chunk == 0:
-            pl.semaphore_wait(barrier, len(greeted))
+    pl.semaphore_wait(barrier, len(greeted))
+    for chunk in range(CHUNKS):
         send(0, chunk)
     loads[2].wait()
     loads[3].wait()

time: 60.6 us -> 60.4 us (level)
  no operation moved by 1% of the time
where the time goes in v5:
time: 60.4 us; the launch traced here: 60.2 us
  Pallas kernels  59.6 us (99%)
  between operations  0.64 us (1%)
    pallas_call x1, Pallas kernels, body(): pl.pallas_call(body_kernel, out_shape=(jax.ShapeDtypeStruct(field, BF), j...  58.8 us

profile of v5, /device:TPU:32, one launch (start us, length us, event | category | flops | bytes accessed | tf_op | source)
XLA Modules:
  0.0 60.2 jit_solution(3431050530293153352)
XLA Ops:
  0.6 58.8 %shard_map.94 = (bf16[16,64,64]{2,1,0:T(8,128)(2,1)S(1)}, bf16[16,64,64]{2,1,0:T(8,128)(2,1)S(1)}, f32[2,32,32]{2,1,0:T(8,128)S(1)}) custom-call(bf16[16,64,64]{2,1,0:T(8,128)(2,1)} %bitcast.11, s32[1,32]{1,0:T(1,128)} %bitcast.15, bf16[16,64,128]{2,1,0:T(8,128)(2,1)} %bitcast.12, bf16[8,16,64,128]{3,2,1,0:T(8,128)(2,1)} %bitcast.9, ...), custom_call_target="tpu_custom_call" | custom-call | tf_op jit(solution)/shard_map/pallas_call | solution.py:423
  59.4 0.8 %shard_map.95 = (bf16[16,64,64]{2,1,0:T(8,128)(2,1)}, bf16[16,64,64]{2,1,0:T(8,128)(2,1)}, f32[2,32,32]{2,1,0:T(8,128)}) custom-call(bf16[16,64,64]{2,1,0:T(8,128)(2,1)S(1)} %get-tuple-element.9.light_in, bf16[16,64,64]{2,1,0:T(8,128)(2,1)S(1)} %get-tuple-element.10.seq_in, f32[2,32,32]{2,1,0:T(8,128)S(1)} %get-tuple-element.11.margin_in), custom_call_target="tpu_custom_call" | custom-call | tf_op jit(solution)/shard_map/pallas_call | solution.py:472
